TPU v7x, 128 devices: a whole 4x4x4 slice. The times are simulated.
128 devices in a mesh: frames: 2 (over core), prow: 8 (over z_lo, x), pcol: 8 (over y, z_hi).
Axes of the slice: x: 4, y: 4, z: 4 (z_hi: 2, z_lo: 2; z = z_hi * 2 + z_lo), core: 2. Of those that a mesh axis runs over, the one named last changes fastest.
Arguments:
- poses: bfloat16 [262144, 256], P(('frames', 'prow', 'pcol')), may hold values from -6 to 6
- codebook: bfloat16 [32, 256], replicated, may hold values from -4 to 4
- offsets: bfloat16 [32, 256], replicated, may hold values from -4 to 4
- confidence: float32 [262144], P(('frames', 'prow', 'pcol')), may hold values from 0.2 to 1
- code_ids: int32 [262144], P(('frames', 'prow', 'pcol')), may hold values from 0 to 31
- creature_ids: int32 [262144], P(('frames', 'prow', 'pcol')), may hold values from 0 to 31
- hess_raw: float32 [8, 8, 128, 8, 8, 128], P(None, 'prow', None, None, 'pcol'), may hold values from -1 to 1, as said below
- pattern: int32 [64, 64], replicated, may hold values from 0 to 1, as said below
- membership: int32 [2, 2], replicated, may hold values from 0 to 63, as said below
Outputs:
- factor_state: float32 [8, 8, 128, 8, 8, 128], P(None, 'prow', None, None, 'pcol')
- reduced_grad: float32 [8, 8, 128], P(None, 'prow')
Inputs may be any that keep to these rules, and one draw needn't show every extreme that they name: As an 8192 x 8192 matrix hess_raw is symmetric. pattern is symmetric with ones on its diagonal. Within each row of membership all pattern entries are one, and for every block row i outside a supernode, pattern[i, p] is the same for all block columns p of that supernode. The 4 entries of membership are distinct block indices.
All inputs are finite; a program needn't handle non-finite values.
Results may differ from a plain program's by a relative error of at most 0.0003.
Values sent between devices are 32-bit elements; how exact they have to be, the bound alone decides.
A program may use at most 64 MiB of HBM per device.

v0:
```python
import math
import jax
import jax.numpy as jnp
from jax import lax
from jax.sharding import PartitionSpec as P

NPAN = 8192
precise = lax.Precision.HIGHEST


def from_root(value, axis, source):
    kept = jnp.where(lax.axis_index(axis) == source, value, 0).astype(value.dtype)
    return lax.psum(kept, axis)


def solve_rows(factor_blk, column):
    blocksize = factor_blk.shape[0]
    block_count = column.shape[0]
    right_side = jnp.transpose(column, (2, 0, 1)).reshape(blocksize, block_count * blocksize)
    solution = jax.scipy.linalg.solve_triangular(factor_blk, right_side, lower=True)
    return jnp.transpose(solution.reshape(blocksize, block_count, blocksize), (1, 2, 0))


def shards(
    poses, codebook, offsets, confidence, code_ids, creature_ids, hess_raw, pattern, membership
):
    grid_rows = lax.axis_size("prow")
    grid_cols = lax.axis_size("pcol")
    my_row = lax.axis_index("prow")
    my_col = lax.axis_index("pcol")
    code_count = codebook.shape[0]
    kind_count = offsets.shape[0]
    local_rows = hess_raw.shape[0]
    local_cols = hess_raw.shape[3]
    blocksize = hess_raw.shape[2]
    code_table = (code_ids[None, :] == jnp.arange(code_count, dtype=jnp.int32)[:, None]).astype(
        jnp.float32
    )
    kind_table = (creature_ids[None, :] == jnp.arange(kind_count, dtype=jnp.int32)[:, None]).astype(
        jnp.float32
    )
    predicted = jnp.einsum("cf,cw->fw", code_table, codebook.astype(jnp.float32), precision=precise)
    predicted = predicted + jnp.einsum(
        "cf,cw->fw", kind_table, offsets.astype(jnp.float32), precision=precise
    )
    residual = confidence[:, None] * (poses.astype(jnp.float32) - predicted)
    frame_total = poses.shape[0] * lax.axis_size("frames") * grid_rows * grid_cols
    partial_grad = jnp.einsum("cf,fw->cw", code_table, residual, precision=precise) / math.sqrt(
        frame_total / code_count
    )
    partial_grad = partial_grad.reshape(local_rows, grid_rows, blocksize)
    summed = lax.psum(partial_grad, ("frames", "prow", "pcol"))
    grad_local = lax.dynamic_index_in_dim(summed, my_row, 1, False)
    shift = 2.5 * math.sqrt(NPAN)
    local_pattern = pattern.reshape(local_rows, grid_rows, local_cols, grid_cols)
    local_pattern = lax.dynamic_index_in_dim(local_pattern, my_row, 1, False)
    local_pattern = lax.dynamic_index_in_dim(local_pattern, my_col, 2, False)
    mask_four = local_pattern.astype(jnp.float32)[:, None, :, None]
    row_ids = jnp.arange(local_rows, dtype=jnp.int32) * grid_rows + my_row
    col_ids = jnp.arange(local_cols, dtype=jnp.int32) * grid_cols + my_col
    same_block = (row_ids[:, None] == col_ids[None, :]).astype(jnp.float32)
    identity = jnp.eye(blocksize, dtype=jnp.float32)
    matrix = (
        hess_raw[:, 0, :, :, 0, :] * mask_four
        + shift * same_block[:, None, :, None] * identity[None, :, None, :]
    )
    order = membership.reshape(-1)

    def eliminate(position, state_pair):
        matrix, grad_local = state_pair
        pivot = order[position]
        pivot_row = pivot % grid_rows
        pivot_col = pivot % grid_cols
        slot_row = pivot // grid_rows
        slot_col = pivot // grid_cols
        on_row = my_row == pivot_row
        on_col = my_col == pivot_col
        diag_here = lax.dynamic_index_in_dim(
            lax.dynamic_index_in_dim(matrix, slot_row, 0, False), slot_col, 1, False
        )
        grad_here = lax.dynamic_index_in_dim(grad_local, slot_row, 0, False)
        diag_blk, grad_blk = (
            from_root(diag_here, ("prow", "pcol"), pivot_row * grid_cols + pivot_col),
            from_root(grad_here, ("prow", "pcol"), pivot_row * grid_cols + pivot_col),
        )
        factor_blk = jnp.linalg.cholesky(diag_blk)
        solved = jax.scipy.linalg.solve_triangular(factor_blk, grad_blk, lower=True)
        column = lax.dynamic_index_in_dim(matrix, slot_col, 2, False)
        column = column * (row_ids != pivot).astype(jnp.float32)[:, None, None]
        panel_rows = from_root(solve_rows(factor_blk, column), "pcol", pivot_col)
        mirrored = from_root(panel_rows, "prow", my_col)
        matrix = matrix - mask_four * jnp.einsum(
            "ixk,jyk->ixjy", panel_rows, mirrored, precision=precise
        )
        grad_local = grad_local - jnp.einsum("ixk,k->ix", panel_rows, solved, precision=precise)
        grad_local = jnp.where(
            on_row, lax.dynamic_update_index_in_dim(grad_local, solved, slot_row, 0), grad_local
        )
        row_block = lax.dynamic_index_in_dim(matrix, slot_row, 0, False)
        matrix = lax.dynamic_update_index_in_dim(
            matrix, jnp.where(on_row, jnp.zeros_like(row_block), row_block), slot_row, 0
        )
        col_block = lax.dynamic_index_in_dim(matrix, slot_col, 2, False)
        filled = jnp.where(
            on_row, lax.dynamic_update_index_in_dim(panel_rows, factor_blk, slot_row, 0), panel_rows
        )
        matrix = lax.dynamic_update_index_in_dim(
            matrix, jnp.where(on_col, filled, col_block), slot_col, 2
        )
        return (matrix, grad_local)

    matrix, grad_local = lax.fori_loop(0, order.shape[0], eliminate, (matrix, grad_local))
    return (matrix[:, None, :, :, None, :], grad_local[:, None, :])


def solution(mesh):
    return jax.shard_map(
        shards,
        mesh=mesh,
        in_specs=(
            P(("frames", "prow", "pcol"), None),
            P(),
            P(),
            P(("frames", "prow", "pcol")),
            P(("frames", "prow", "pcol")),
            P(("frames", "prow", "pcol")),
            P(None, "prow", None, None, "pcol", None),
            P(),
            P(),
        ),
        out_specs=(P(None, "prow", None, None, "pcol", None), P(None, "prow", None)),
        check_vma=False,
    )
```

profile of v0, /device:TPU:0, one launch (start us, length us, event | category | flops | bytes accessed | tf_op | source)
XLA Modules:
  0.0 1798.9 jit_solution(806905055227306704)
XLA Ops:
  9.2 1.2 fusion.17
  10.4 2.0 fusion.16
  13.3 68.3 %psum.67 = f32[8,8,128]{2,1,0:T(8,128)S(1)} all-reduce(f32[8,8,128]{2,1,0:T(8,128)S(1)} %reshape.143), channel_id=1, replica_groups=mesh['frames'=2,'prow'=8,'pcol'=8] {'frames','prow','pcol'}, use_global_device_ids=true, to_apply=%region_0.0 | all-reduce | flops 8192 | bytes 65536 | tf_op jit(solution)/shard_map/psum | solution.py:52
  81.7 10.9 copy.33
  92.5 4.7 fusion.14
  97.2 1689.5 %while.20 = (s32[]{:T(128)}, f32[8,128,8,128]{1,3,2,0:T(8,128)}, f32[8,128]{1,0:T(8,128)S(1)}, f32[8,1,8,1]{2,0,3,1:T(8,128)S(1)}, s32[4]{0:T(128)S(1)}, /*index...) while((s32[]{:T(128)}, f32[8,128,8,128]{1,3,2,0:T(8,128)}, ...), condition=%wide.region_8.9_spmd.clone.clone, body=%wide.region_1.8_spmd.clone.clone.sunk | while | flops 1816970880 | bytes 44392472 | solution.py:112
  100.1 1.5 select_bitcast_fusion.4
  101.6 1.1 constant_dynamic-slice_fusion.7
  103.5 117.8 %all-reduce.4.cloned.1.call-done = f32[128,128]{0,1:T(8,128)} async-done(((f32[128,128]{0,1:T(8,128)}), f32[128,128]{0,1:T(8,128)}) %all-reduce.4.cloned.1.call-update) | async-done | bytes 65552 | tf_op jit(solution)/shard_map/while/body/eval_jaxpr/psum | solution.py:13
  223.1 11.7 cholesky.80
  236.3 9.8 custom-call.29
  246.1 1.4 convolution_select_fusion.2
  247.6 5.3 copy.44
  253.0 176.0 %psum.83 = f32[128]{0:T(128)S(1)} all-reduce(f32[128]{0:T(128)S(1)} %fusion.50), channel_id=1, replica_groups=mesh['frames'=2,'prow'=8,'pcol'=8] {'prow','pcol'}, use_global_device_ids=true, to_apply=%region_7.7 | all-reduce | flops 128 | bytes 1024 | tf_op jit(solution)/shard_map/while/body/eval_jaxpr/psum | solution.py:13
  429.0 1.9 broadcast_select_fusion.5
  431.0 1.6 fusion.52
  432.7 66.4 %all-reduce.8.cloned.1.call-done = f32[8,128,128]{2,1,0:T(8,128)} async-done(((f32[8,128,128]{2,1,0:T(8,128)}), f32[8,128,128]{2,1,0:T(8,128)}) %all-reduce.8.cloned.1.call-update) | async-done | bytes 524304 | tf_op jit(solution)/shard_map/while/body/eval_jaxpr/psum | solution.py:13
  499.1 8.2 multiply_subtract_fusion.2
  507.3 1.9 select_dynamic-update-slice_fusion.2
  509.2 1.1 constant_dynamic-slice_fusion.8
  511.8 5.3 copy.47
  520.0 1.5 select_bitcast_fusion.4
  521.6 1.1 constant_dynamic-slice_fusion.7
  523.4 120.9 %all-reduce.4.cloned.1.call-done = f32[128,128]{0,1:T(8,128)} async-done(((f32[128,128]{0,1:T(8,128)}), f32[128,128]{0,1:T(8,128)}) %all-reduce.4.cloned.1.call-update) | async-done | bytes 65552 | tf_op jit(solution)/shard_map/while/body/eval_jaxpr/psum | solution.py:13
  646.1 11.7 cholesky.80
  659.3 9.8 custom-call.29
  669.1 1.4 convolution_select_fusion.2
  670.6 5.3 copy.44
  676.0 176.0 %psum.83 = f32[128]{0:T(128)S(1)} all-reduce(f32[128]{0:T(128)S(1)} %fusion.50), channel_id=1, replica_groups=mesh['frames'=2,'prow'=8,'pcol'=8] {'prow','pcol'}, use_global_device_ids=true, to_apply=%region_7.7 | all-reduce | flops 128 | bytes 1024 | tf_op jit(solution)/shard_map/while/body/eval_jaxpr/psum | solution.py:13
  852.0 1.9 broadcast_select_fusion.5
  854.1 1.6 fusion.52
  855.8 66.4 %all-reduce.8.cloned.1.call-done = f32[8,128,128]{2,1,0:T(8,128)} async-done(((f32[8,128,128]{2,1,0:T(8,128)}), f32[8,128,128]{2,1,0:T(8,128)}) %all-reduce.8.cloned.1.call-update) | async-done | bytes 524304 | tf_op jit(solution)/shard_map/while/body/eval_jaxpr/psum | solution.py:13
  922.2 8.2 multiply_subtract_fusion.2
  930.4 1.9 select_dynamic-update-slice_fusion.2
  934.9 5.3 copy.47
  943.1 1.5 select_bitcast_fusion.4
  944.7 1.1 constant_dynamic-slice_fusion.7
  946.5 121.1 %all-reduce.4.cloned.1.call-done = f32[128,128]{0,1:T(8,128)} async-done(((f32[128,128]{0,1:T(8,128)}), f32[128,128]{0,1:T(8,128)}) %all-reduce.4.cloned.1.call-update) | async-done | bytes 65552 | tf_op jit(solution)/shard_map/while/body/eval_jaxpr/psum | solution.py:13
  1069.5 11.7 cholesky.80
  1082.6 9.8 custom-call.29
  1092.5 1.4 convolution_select_fusion.2
  1094.0 5.3 copy.44
  1099.3 176.0 %psum.83 = f32[128]{0:T(128)S(1)} all-reduce(f32[128]{0:T(128)S(1)} %fusion.50), channel_id=1, replica_groups=mesh['frames'=2,'prow'=8,'pcol'=8] {'prow','pcol'}, use_global_device_ids=true, to_apply=%region_7.7 | all-reduce | flops 128 | bytes 1024 | tf_op jit(solution)/shard_map/while/body/eval_jaxpr/psum | solution.py:13
  1275.3 1.9 broadcast_select_fusion.5
  1277.4 1.6 fusion.52
  1279.1 66.4 %all-reduce.8.cloned.1.call-done = f32[8,128,128]{2,1,0:T(8,128)} async-done(((f32[8,128,128]{2,1,0:T(8,128)}), f32[8,128,128]{2,1,0:T(8,128)}) %all-reduce.8.cloned.1.call-update) | async-done | bytes 524304 | tf_op jit(solution)/shard_map/while/body/eval_jaxpr/psum | solution.py:13
  1345.5 8.2 multiply_subtract_fusion.2
  1353.7 1.9 select_dynamic-update-slice_fusion.2
  1358.2 5.3 copy.47
  1366.4 1.5 select_bitcast_fusion.4
  1368.0 1.1 constant_dynamic-slice_fusion.7
  1369.8 120.9 %all-reduce.4.cloned.1.call-done = f32[128,128]{0,1:T(8,128)} async-done(((f32[128,128]{0,1:T(8,128)}), f32[128,128]{0,1:T(8,128)}) %all-reduce.4.cloned.1.call-update) | async-done | bytes 65552 | tf_op jit(solution)/shard_map/while/body/eval_jaxpr/psum | solution.py:13
  1492.5 11.7 cholesky.80
  1505.7 9.8 custom-call.29
  1515.5 1.4 convolution_select_fusion.2
  1517.0 5.3 copy.44
  1522.4 176.0 %psum.83 = f32[128]{0:T(128)S(1)} all-reduce(f32[128]{0:T(128)S(1)} %fusion.50), channel_id=1, replica_groups=mesh['frames'=2,'prow'=8,'pcol'=8] {'prow','pcol'}, use_global_device_ids=true, to_apply=%region_7.7 | all-reduce | flops 128 | bytes 1024 | tf_op jit(solution)/shard_map/while/body/eval_jaxpr/psum | solution.py:13
  1698.4 1.9 broadcast_select_fusion.5
  1700.5 1.6 fusion.52
  1702.1 66.5 %all-reduce.8.cloned.1.call-done = f32[8,128,128]{2,1,0:T(8,128)} async-done(((f32[8,128,128]{2,1,0:T(8,128)}), f32[8,128,128]{2,1,0:T(8,128)}) %all-reduce.8.cloned.1.call-update) | async-done | bytes 524304 | tf_op jit(solution)/shard_map/while/body/eval_jaxpr/psum | solution.py:13
  1768.6 8.2 multiply_subtract_fusion.2
  1776.8 1.9 select_dynamic-update-slice_fusion.2
  1781.3 5.3 copy.47
  1786.7 5.3 copy.35
  (115 shorter events, 32.2 us)
Async XLA Ops:
  7.2 2.1 copy-start
  7.2 5.2 copy-start.3
  97.2 124.1 %all-reduce.4.cloned.1.call-start = ((), (), s32[]{:S(2)}) async-start(), calls=%async_computation | async-start | bytes 131072 | tf_op jit(solution)/shard_map/while/body/eval_jaxpr/psum | solution.py:13
  101.6 327.4 %all-reduce.6.cloned.1.call-start = ((), (), s32[]{:S(2)}) async-start(), calls=%async_computation.1 | async-start | bytes 1048576 | tf_op jit(solution)/shard_map/while/body/eval_jaxpr/psum | solution.py:13
  247.5 251.6 %all-reduce.8.cloned.1.call-start = ((), (), s32[]{:S(2)}) async-start(), calls=%async_computation.2 | async-start | bytes 1048576 | tf_op jit(solution)/shard_map/while/body/eval_jaxpr/psum | solution.py:13
  499.1 11.1 copy-start.1
  517.2 127.1 %all-reduce.4.cloned.1.call-start = ((), (), s32[]{:S(2)}) async-start(), calls=%async_computation | async-start | bytes 131072 | tf_op jit(solution)/shard_map/while/body/eval_jaxpr/psum | solution.py:13
  521.5 330.5 %all-reduce.6.cloned.1.call-start = ((), (), s32[]{:S(2)}) async-start(), calls=%async_computation.1 | async-start | bytes 1048576 | tf_op jit(solution)/shard_map/while/body/eval_jaxpr/psum | solution.py:13
  670.6 251.6 %all-reduce.8.cloned.1.call-start = ((), (), s32[]{:S(2)}) async-start(), calls=%async_computation.2 | async-start | bytes 1048576 | tf_op jit(solution)/shard_map/while/body/eval_jaxpr/psum | solution.py:13
  922.2 11.1 copy-start.1
  940.2 127.4 %all-reduce.4.cloned.1.call-start = ((), (), s32[]{:S(2)}) async-start(), calls=%async_computation | async-start | bytes 131072 | tf_op jit(solution)/shard_map/while/body/eval_jaxpr/psum | solution.py:13
  944.6 330.7 %all-reduce.6.cloned.1.call-start = ((), (), s32[]{:S(2)}) async-start(), calls=%async_computation.1 | async-start | bytes 1048576 | tf_op jit(solution)/shard_map/while/body/eval_jaxpr/psum | solution.py:13
  1093.9 251.6 %all-reduce.8.cloned.1.call-start = ((), (), s32[]{:S(2)}) async-start(), calls=%async_computation.2 | async-start | bytes 1048576 | tf_op jit(solution)/shard_map/while/body/eval_jaxpr/psum | solution.py:13
  1345.5 11.1 copy-start.1
  1363.5 127.1 %all-reduce.4.cloned.1.call-start = ((), (), s32[]{:S(2)}) async-start(), calls=%async_computation | async-start | bytes 131072 | tf_op jit(solution)/shard_map/while/body/eval_jaxpr/psum | solution.py:13
  1367.9 330.5 %all-reduce.6.cloned.1.call-start = ((), (), s32[]{:S(2)}) async-start(), calls=%async_computation.1 | async-start | bytes 1048576 | tf_op jit(solution)/shard_map/while/body/eval_jaxpr/psum | solution.py:13
  1516.9 251.7 %all-reduce.8.cloned.1.call-start = ((), (), s32[]{:S(2)}) async-start(), calls=%async_computation.2 | async-start | bytes 1048576 | tf_op jit(solution)/shard_map/while/body/eval_jaxpr/psum | solution.py:13
  1768.6 11.1 copy-start.1
  1786.7 5.3 copy-start.2
Sparse Core Ops, SparseCore 0:
  103.3 117.9 all-reduce.3
  247.7 83.5 all-reduce.5
  431.0 68.0 all-reduce.7
  522.9 121.3 all-reduce.3
  670.7 83.5 all-reduce.5
  854.0 68.0 all-reduce.7
  946.3 121.2 all-reduce.3
  1094.0 83.5 all-reduce.5
  1277.4 68.0 all-reduce.7
  1369.3 121.3 all-reduce.3
  1517.1 83.5 all-reduce.5
  1700.4 68.1 all-reduce.7
where the time goes:
time: 1800 us
  blocking collectives  772 us (43%)
  waiting for transfers between devices  747 us (42%)
  other arithmetic  130 us (7%)
  local copies, waits for them, and re-layouts  76.4 us (4%)
  matrix products  49.5 us (3%)
    psum x12, waiting for transfers between devices, from_root(): return lax.psum(kept, axis)  746 us
    psum x4, blocking collectives, from_root(): return lax.psum(kept, axis)  704 us
    psum x1, blocking collectives, shards(): summed = lax.psum(partial_grad, ('frames', 'prow', 'pcol'))  68.3 us
    another operation x12, other arithmetic, eliminate(): factor_blk = jnp.linalg.cholesky(diag_blk)  49.9 us
    while x16, local copies, waits for them, and re-layouts  42.8 us
    another operation x8, other arithmetic, solve_rows(): jax.scipy.linalg.solve_triangular(factor_blk, right_side, lower=True)  42 us
  transfers between devices with their start and end apart: 12, of which 8 were waited for; matrix products, arithmetic and copies ran while one was open for 2% of the time, Pallas kernels for 0%

commit v1 on v0

--- a/solution.py
+++ b/solution.py
@@ -49,7 +49,12 @@
         frame_total / code_count
     )
     partial_grad = partial_grad.reshape(local_rows, grid_rows, blocksize)
-    summed = lax.psum(partial_grad, ("frames", "prow", "pcol"))
+
+    def render_windows(array_in):
+        local_part = jax.lax.all_gather(array_in, axis_name=("frames", "prow", "pcol")).sum(axis=0)
+        return local_part
+
+    summed = render_windows(partial_grad)
     grad_local = lax.dynamic_index_in_dim(summed, my_row, 1, False)
     shift = 2.5 * math.sqrt(NPAN)
     local_pattern = pattern.reshape(local_rows, grid_rows, local_cols, grid_cols)

time: 1800 us -> 1920 us (1.067)
  waiting for transfers between devices: 747 us -> 934 us
  blocking collectives: 772 us -> 704 us
    all_gather x0 -> x1, waiting for transfers between devices: none -> 185 us  [render_windows(): jax.lax.all_gather(array_in, axis_name=('frames', 'prow', 'pcol'))]
    psum x1 -> x0, blocking collectives: 68.3 us -> none  [shards(): summed = lax.psum(partial_grad, ('frames', 'prow', 'pcol'))]
  transfers between devices with their start and end apart: 12 -> 13, of which waited for: 8 -> 9; matrix products, arithmetic and copies ran while one was open for 2% -> 3% of each run, Pallas kernels for 0% -> 0%
where the time goes in v1:
time: 1920 us
  waiting for transfers between devices  934 us (49%)
  blocking collectives  704 us (37%)
  other arithmetic  131 us (7%)
  local copies, waits for them, and re-layouts  76.1 us (4%)
  matrix products  49.5 us (3%)
    psum x12, waiting for transfers between devices, from_root(): return lax.psum(kept, axis)  749 us
    psum x4, blocking collectives, from_root(): return lax.psum(kept, axis)  704 us
    all_gather x1, waiting for transfers between devices, render_windows(): jax.lax.all_gather(array_in, axis_name=('frames', 'prow', 'pcol'))  185 us
    another operation x12, other arithmetic, eliminate(): factor_blk = jnp.linalg.cholesky(diag_blk)  49.4 us
    while x16, local copies, waits for them, and re-layouts  42.8 us
    another operation x8, other arithmetic, solve_rows(): jax.scipy.linalg.solve_triangular(factor_blk, right_side, lower=True)  41.6 us
  transfers between devices with their start and end apart: 13, of which 9 were waited for; matrix products, arithmetic and copies ran while one was open for 3% of the time, Pallas kernels for 0%

profile of v1, /device:TPU:0, one launch (start us, length us, event | category | flops | bytes accessed | tf_op | source)
XLA Modules:
  0.0 1919.2 jit_solution(5506662451103007685)
XLA Ops:
  7.9 1.2 fusion.17
  9.1 2.0 fusion.16
  13.1 10.9 copy.42
  24.1 4.7 fusion.14
  28.8 185.0 %all-gather.2.cloned.1.call-done = f32[128,8,8,128]{3,2,1,0:T(8,128)} async-done(((f32[1,8,8,128]{3,2,1,0:T(8,128)}), f32[128,8,8,128]{3,2,1,0:T(8,128)}) %all-gather.2.cloned.1.call-update) | async-done | bytes 4194320 | tf_op jit(solution)/shard_map/all_gather | solution.py:54
  213.8 2.5 reduce_sum.9
  216.3 1691.0 %while.20 = (s32[]{:T(128)}, f32[8,128,8,128]{1,3,2,0:T(8,128)}, f32[8,128]{1,0:T(8,128)S(1)}, f32[8,1,8,1]{2,0,3,1:T(8,128)S(1)}, s32[4]{0:T(128)S(1)}, /*index...) while((s32[]{:T(128)}, f32[8,128,8,128]{1,3,2,0:T(8,128)}, ...), condition=%wide.region_8.9_spmd.clone.clone, body=%wide.region_1.8_spmd.clone.clone.sunk | while | flops 1816970880 | bytes 44392472 | solution.py:117
  219.4 1.5 select_bitcast_fusion.4
  221.0 1.1 constant_dynamic-slice_fusion.7
  222.9 119.8 %all-reduce.4.cloned.1.call-done = f32[128,128]{0,1:T(8,128)} async-done(((f32[128,128]{0,1:T(8,128)}), f32[128,128]{0,1:T(8,128)}) %all-reduce.4.cloned.1.call-update) | async-done | bytes 65552 | tf_op jit(solution)/shard_map/while/body/eval_jaxpr/psum | solution.py:13
  344.5 11.7 cholesky.80
  357.4 9.8 custom-call.29
  367.2 1.4 convolution_select_fusion.2
  368.8 5.3 copy.53
  374.1 176.0 %psum.75 = f32[128]{0:T(128)S(1)} all-reduce(f32[128]{0:T(128)S(1)} %fusion.50), channel_id=1, replica_groups=mesh['frames'=2,'prow'=8,'pcol'=8] {'prow','pcol'}, use_global_device_ids=true, to_apply=%region_7.7 | all-reduce | flops 128 | bytes 1024 | tf_op jit(solution)/shard_map/while/body/eval_jaxpr/psum | solution.py:13
  550.1 1.9 broadcast_select_fusion.5
  552.2 1.6 fusion.52
  553.9 66.6 %all-reduce.8.cloned.1.call-done = f32[8,128,128]{2,1,0:T(8,128)} async-done(((f32[8,128,128]{2,1,0:T(8,128)}), f32[8,128,128]{2,1,0:T(8,128)}) %all-reduce.8.cloned.1.call-update) | async-done | bytes 524304 | tf_op jit(solution)/shard_map/while/body/eval_jaxpr/psum | solution.py:13
  620.5 8.2 multiply_subtract_fusion.2
  628.6 1.9 select_dynamic-update-slice_fusion.2
  633.1 5.3 copy.56
  641.3 1.5 select_bitcast_fusion.4
  642.8 1.1 constant_dynamic-slice_fusion.7
  644.7 120.8 %all-reduce.4.cloned.1.call-done = f32[128,128]{0,1:T(8,128)} async-done(((f32[128,128]{0,1:T(8,128)}), f32[128,128]{0,1:T(8,128)}) %all-reduce.4.cloned.1.call-update) | async-done | bytes 65552 | tf_op jit(solution)/shard_map/while/body/eval_jaxpr/psum | solution.py:13
  767.3 11.7 cholesky.80
  780.2 9.8 custom-call.29
  790.0 1.4 convolution_select_fusion.2
  791.6 5.3 copy.53
  796.9 176.0 %psum.75 = f32[128]{0:T(128)S(1)} all-reduce(f32[128]{0:T(128)S(1)} %fusion.50), channel_id=1, replica_groups=mesh['frames'=2,'prow'=8,'pcol'=8] {'prow','pcol'}, use_global_device_ids=true, to_apply=%region_7.7 | all-reduce | flops 128 | bytes 1024 | tf_op jit(solution)/shard_map/while/body/eval_jaxpr/psum | solution.py:13
  973.0 1.9 broadcast_select_fusion.5
  975.0 1.6 fusion.52
  976.7 66.4 %all-reduce.8.cloned.1.call-done = f32[8,128,128]{2,1,0:T(8,128)} async-done(((f32[8,128,128]{2,1,0:T(8,128)}), f32[8,128,128]{2,1,0:T(8,128)}) %all-reduce.8.cloned.1.call-update) | async-done | bytes 524304 | tf_op jit(solution)/shard_map/while/body/eval_jaxpr/psum | solution.py:13
  1043.1 8.2 multiply_subtract_fusion.2
  1051.3 1.9 select_dynamic-update-slice_fusion.2
  1055.7 5.3 copy.56
  1063.9 1.5 select_bitcast_fusion.4
  1065.5 1.1 constant_dynamic-slice_fusion.7
  1067.4 121.1 %all-reduce.4.cloned.1.call-done = f32[128,128]{0,1:T(8,128)} async-done(((f32[128,128]{0,1:T(8,128)}), f32[128,128]{0,1:T(8,128)}) %all-reduce.4.cloned.1.call-update) | async-done | bytes 65552 | tf_op jit(solution)/shard_map/while/body/eval_jaxpr/psum | solution.py:13
  1190.3 11.7 cholesky.80
  1203.2 9.8 custom-call.29
  1213.0 1.4 convolution_select_fusion.2
  1214.6 5.3 copy.53
  1219.9 176.0 %psum.75 = f32[128]{0:T(128)S(1)} all-reduce(f32[128]{0:T(128)S(1)} %fusion.50), channel_id=1, replica_groups=mesh['frames'=2,'prow'=8,'pcol'=8] {'prow','pcol'}, use_global_device_ids=true, to_apply=%region_7.7 | all-reduce | flops 128 | bytes 1024 | tf_op jit(solution)/shard_map/while/body/eval_jaxpr/psum | solution.py:13
  1396.0 1.9 broadcast_select_fusion.5
  1398.0 1.6 fusion.52
  1399.7 66.5 %all-reduce.8.cloned.1.call-done = f32[8,128,128]{2,1,0:T(8,128)} async-done(((f32[8,128,128]{2,1,0:T(8,128)}), f32[8,128,128]{2,1,0:T(8,128)}) %all-reduce.8.cloned.1.call-update) | async-done | bytes 524304 | tf_op jit(solution)/shard_map/while/body/eval_jaxpr/psum | solution.py:13
  1466.2 8.2 multiply_subtract_fusion.2
  1474.4 1.9 select_dynamic-update-slice_fusion.2
  1478.8 5.3 copy.56
  1487.0 1.5 select_bitcast_fusion.4
  1488.6 1.1 constant_dynamic-slice_fusion.7
  1490.4 121.1 %all-reduce.4.cloned.1.call-done = f32[128,128]{0,1:T(8,128)} async-done(((f32[128,128]{0,1:T(8,128)}), f32[128,128]{0,1:T(8,128)}) %all-reduce.4.cloned.1.call-update) | async-done | bytes 65552 | tf_op jit(solution)/shard_map/while/body/eval_jaxpr/psum | solution.py:13
  1613.3 11.7 cholesky.80
  1626.3 9.8 custom-call.29
  1636.1 1.4 convolution_select_fusion.2
  1637.6 5.3 copy.53
  1643.0 176.1 %psum.75 = f32[128]{0:T(128)S(1)} all-reduce(f32[128]{0:T(128)S(1)} %fusion.50), channel_id=1, replica_groups=mesh['frames'=2,'prow'=8,'pcol'=8] {'prow','pcol'}, use_global_device_ids=true, to_apply=%region_7.7 | all-reduce | flops 128 | bytes 1024 | tf_op jit(solution)/shard_map/while/body/eval_jaxpr/psum | solution.py:13
  1819.0 1.9 broadcast_select_fusion.5
  1821.1 1.6 fusion.52
  1822.8 66.6 %all-reduce.8.cloned.1.call-done = f32[8,128,128]{2,1,0:T(8,128)} async-done(((f32[8,128,128]{2,1,0:T(8,128)}), f32[8,128,128]{2,1,0:T(8,128)}) %all-reduce.8.cloned.1.call-update) | async-done | bytes 524304 | tf_op jit(solution)/shard_map/while/body/eval_jaxpr/psum | solution.py:13
  1889.4 8.2 multiply_subtract_fusion.2
  1897.5 1.9 select_dynamic-update-slice_fusion.2
  1901.9 5.3 copy.56
  1907.3 5.3 copy.44
  (122 shorter events, 31.7 us)
Async XLA Ops:
  7.2 0.7 copy-start
  7.2 3.9 copy-start.3
  7.2 206.6 %all-gather.2.cloned.1.call-start = ((), (), s32[]{:S(2)}) async-start(), calls=%async_computation | async-start | bytes 4227072 | tf_op jit(solution)/shard_map/all_gather | solution.py:54
  9.1 3.6 copy-start.5
  9.1 3.6 copy-start.4
  216.5 126.2 %all-reduce.4.cloned.1.call-start = ((), (), s32[]{:S(2)}) async-start(), calls=%async_computation.1 | async-start | bytes 131072 | tf_op jit(solution)/shard_map/while/body/eval_jaxpr/psum | solution.py:13
  220.9 329.2 %all-reduce.6.cloned.1.call-start = ((), (), s32[]{:S(2)}) async-start(), calls=%async_computation.2 | async-start | bytes 1048576 | tf_op jit(solution)/shard_map/while/body/eval_jaxpr/psum | solution.py:13
  368.7 251.8 %all-reduce.8.cloned.1.call-start = ((), (), s32[]{:S(2)}) async-start(), calls=%async_computation.3 | async-start | bytes 1048576 | tf_op jit(solution)/shard_map/while/body/eval_jaxpr/psum | solution.py:13
  620.5 11.1 copy-start.1
  638.4 127.1 %all-reduce.4.cloned.1.call-start = ((), (), s32[]{:S(2)}) async-start(), calls=%async_computation.1 | async-start | bytes 131072 | tf_op jit(solution)/shard_map/while/body/eval_jaxpr/psum | solution.py:13
  642.8 330.2 %all-reduce.6.cloned.1.call-start = ((), (), s32[]{:S(2)}) async-start(), calls=%async_computation.2 | async-start | bytes 1048576 | tf_op jit(solution)/shard_map/while/body/eval_jaxpr/psum | solution.py:13
  791.5 251.6 %all-reduce.8.cloned.1.call-start = ((), (), s32[]{:S(2)}) async-start(), calls=%async_computation.3 | async-start | bytes 1048576 | tf_op jit(solution)/shard_map/while/body/eval_jaxpr/psum | solution.py:13
  1043.1 11.1 copy-start.1
  1061.1 127.4 %all-reduce.4.cloned.1.call-start = ((), (), s32[]{:S(2)}) async-start(), calls=%async_computation.1 | async-start | bytes 131072 | tf_op jit(solution)/shard_map/while/body/eval_jaxpr/psum | solution.py:13
  1065.4 330.5 %all-reduce.6.cloned.1.call-start = ((), (), s32[]{:S(2)}) async-start(), calls=%async_computation.2 | async-start | bytes 1048576 | tf_op jit(solution)/shard_map/while/body/eval_jaxpr/psum | solution.py:13
  1214.5 251.7 %all-reduce.8.cloned.1.call-start = ((), (), s32[]{:S(2)}) async-start(), calls=%async_computation.3 | async-start | bytes 1048576 | tf_op jit(solution)/shard_map/while/body/eval_jaxpr/psum | solution.py:13
  1466.2 11.1 copy-start.1
  1484.1 127.4 %all-reduce.4.cloned.1.call-start = ((), (), s32[]{:S(2)}) async-start(), calls=%async_computation.1 | async-start | bytes 131072 | tf_op jit(solution)/shard_map/while/body/eval_jaxpr/psum | solution.py:13
  1488.5 330.5 %all-reduce.6.cloned.1.call-start = ((), (), s32[]{:S(2)}) async-start(), calls=%async_computation.2 | async-start | bytes 1048576 | tf_op jit(solution)/shard_map/while/body/eval_jaxpr/psum | solution.py:13
  1637.5 251.8 %all-reduce.8.cloned.1.call-start = ((), (), s32[]{:S(2)}) async-start(), calls=%async_computation.3 | async-start | bytes 1048576 | tf_op jit(solution)/shard_map/while/body/eval_jaxpr/psum | solution.py:13
  1889.4 11.1 copy-start.1
  1907.3 5.3 copy-start.2
Sparse Core Ops, SparseCore 0:
  12.7 201.0 all-gather.1
  222.6 120.0 all-reduce.3
  368.8 83.5 all-reduce.5
  552.2 68.2 all-reduce.7
  644.2 121.2 all-reduce.3
  791.6 83.5 all-reduce.5
  975.0 68.0 all-reduce.7
  1067.2 121.2 all-reduce.3
  1214.6 83.5 all-reduce.5
  1398.0 68.1 all-reduce.7
  1490.2 121.2 all-reduce.3
  1637.7 83.5 all-reduce.5
  1821.1 68.2 all-reduce.7
